TPU v7x, 256 devices: a whole 4x4x8 slice. The times are simulated.
256 devices in a mesh: star: 64 (over y, z_lo, x, core), gas: 4 (over z_hi).
Axes of the slice: x: 4, y: 4, z: 8 (z_hi: 4, z_lo: 2; z = z_hi * 2 + z_lo), core: 2. Of those that a mesh axis runs over, the one named last changes fastest.
Arguments:
- star_pos: float32 [3, 131072], P(None, ('star', 'gas')), may hold values from 0 to 32
- star_vel: float32 [3, 131072], P(None, ('star', 'gas')), may hold values from -6 to 6
- star_accel: float32 [6, 131072], P(None, ('star', 'gas')), may hold values from -6 to 6
- star_mass: float32 [131072], P(('star', 'gas')), may hold values from 0.1 to 2
- active: int32 [2048], replicated, may hold values from 0 to 131071, as said below
- density: float32 [256, 32, 64], P('star', 'gas'), may hold values from 0.5 to 4
- flow_in: float32 [3, 256, 32, 64], P(None, 'star', 'gas'), may hold values from -2 to 2
- field_in: float32 [3, 256, 32, 64], P(None, 'star', 'gas'), may hold values from -4 to 4
Outputs:
- star_new: float32 [12, 131072], P(None, ('star', 'gas'))
- flow: float32 [3, 256, 32, 64], P(None, 'star', 'gas')
- field_out: float32 [3, 256, 32, 64], P(None, 'star', 'gas')
Inputs may be any that keep to these rules, and one draw needn't show every extreme that they name: Distinct and increasing; among the 512 consecutive indices of one device at most 24 are active, and in every draw some device holds exactly 24.
All inputs are finite; a program needn't handle non-finite values.
Results may differ from a plain program's by a relative error of at most 0.0001.
Values sent between devices are 32-bit elements; how exact they have to be, the bound alone decides.
A program may use at most 64 MiB of HBM per device.

v0:
```python
import math
import jax
import jax.numpy as jnp
from jax import lax
from jax.sharding import PartitionSpec as P

MOST = 24
gravity = 0.02
soften = 4.0
time_step = 1.5
field_step = 0.1
highest = lax.Precision.HIGHEST


def with_halo(block, sides, width):
    for axis, dim in sides:
        count = lax.axis_size(axis)
        forward = [(i, i + 1) for i in range(count - 1)]
        forward.append((count - 1, 0))
        backward = [(target, source) for source, target in forward]
        low = lax.ppermute(
            lax.slice_in_dim(block, block.shape[dim] - width, None, axis=dim), axis, forward
        )
        high = lax.ppermute(lax.slice_in_dim(block, 0, width, axis=dim), axis, backward)
        block = jnp.concatenate([low, block, high], axis=dim)
    return block


def grad_x(values):
    return 0.5 * (values[2:, 1:-1] - values[:-2, 1:-1])


def grad_y(values):
    return 0.5 * (values[1:-1, 2:] - values[1:-1, :-2])


def grad_z(values):
    return 0.5 * (jnp.roll(values, -1, 2) - jnp.roll(values, 1, 2))[1:-1, 1:-1]


def trim_rim(values):
    return values[1:-1, 1:-1]


def curl_of(comp_a, comp_b, comp_c):
    return (
        grad_y(comp_c) - grad_z(comp_b),
        grad_z(comp_a) - grad_x(comp_c),
        grad_x(comp_b) - grad_y(comp_a),
    )


def cross_of(lhs_vec, rhs_vec):
    return (
        lhs_vec[1] * rhs_vec[2] - lhs_vec[2] * rhs_vec[1],
        lhs_vec[2] * rhs_vec[0] - lhs_vec[0] * rhs_vec[2],
        lhs_vec[0] * rhs_vec[1] - lhs_vec[1] * rhs_vec[0],
    )


def field_rate(padded_field, padded_flow, padded_density):
    current = curl_of(padded_field[0], padded_field[1], padded_field[2])
    inner_field = (trim_rim(padded_field[0]), trim_rim(padded_field[1]), trim_rim(padded_field[2]))
    inner_flow = (trim_rim(padded_flow[0]), trim_rim(padded_flow[1]), trim_rim(padded_flow[2]))
    resist = trim_rim(padded_density) ** (-1.5)
    lorentz = cross_of(current, inner_field)
    drift = cross_of(lorentz, inner_field)
    motion = cross_of(inner_flow, inner_field)
    emf_a = motion[0] + resist * drift[0]
    emf_b = motion[1] + resist * drift[1]
    emf_c = motion[2] + resist * drift[2]
    return jnp.stack(curl_of(emf_a, emf_b, emf_c))


def pair_terms(target, resident, cell_place, cell_mass):
    star_gap = resident[0:3, None, :] - target[0:3, :, None]
    rel_vel = resident[3:6, None, :] - target[3:6, :, None]
    inv_r = lax.rsqrt(jnp.sum(star_gap * star_gap, 0) + soften)
    weight = gravity * resident[6][None, :] * inv_r * inv_r * inv_r
    star_acc = jnp.sum(weight[None] * star_gap, 2)
    approach = jnp.sum(star_gap * rel_vel, 0)
    star_jerk = jnp.sum(
        weight[None] * (rel_vel - 3.0 * (approach * inv_r * inv_r)[None] * star_gap), 2
    )
    cell_gap = cell_place[:, None, :] - target[0:3, :, None]
    inv_g = lax.rsqrt(jnp.sum(cell_gap * cell_gap, 0) + soften)
    inv_cube = gravity * inv_g * inv_g * inv_g
    gas_acc = jnp.sum((inv_cube * cell_mass[None, :])[None] * cell_gap, 2)
    cell_kick = -jnp.sum((inv_cube * target[6][:, None])[None] * cell_gap, 1)
    return (jnp.concatenate([star_acc + gas_acc, star_jerk], 0), cell_kick)


def all_terms(targets, resident, cell_place, cell_mass):
    target_total = targets.shape[1]
    block_width = math.gcd(target_total, 64)
    blocks = targets.reshape(7, target_total // block_width, block_width).transpose(1, 0, 2)

    def one_block(running, target_block):
        terms_here, cell_kick = pair_terms(target_block, resident, cell_place, cell_mass)
        return (running + cell_kick, terms_here)

    kick_sum, block_terms = lax.scan(one_block, jnp.zeros(cell_place.shape, jnp.float32), blocks)
    return (block_terms.transpose(1, 0, 2).reshape(6, target_total), kick_sum)


def body(star_pos, star_vel, star_accel, star_mass, active, density, flow_in, field_in):
    resident_total = star_pos.shape[1]
    old_acc = star_accel[0:3]
    old_jerk = star_accel[3:6]
    pred_pos = (
        star_pos
        + time_step * star_vel
        + time_step**2 / 2.0 * old_acc
        + time_step**3 / 6.0 * old_jerk
    )
    pred_vel = star_vel + time_step * old_acc + time_step**2 / 2.0 * old_jerk
    resident = jnp.concatenate([pred_pos, pred_vel, star_mass[None]], 0)
    my_rank = lax.axis_index("star") * lax.axis_size("gas") + lax.axis_index("gas")
    owner_of = active // resident_total
    local_slot = active % resident_total
    is_mine = owner_of == my_rank
    rows_iota = jnp.arange(resident_total, dtype=jnp.int32)
    owned = (is_mine[None, :] & (local_slot[None, :] == rows_iota[:, None])).astype(jnp.float32)
    active_mask = jnp.sum(owned, 1) > 0.5
    ext_x, ext_y, ext_z = density.shape
    grid_shape = (ext_x, ext_y, ext_z)
    coord_x = (lax.axis_index("star") * ext_x + jnp.arange(ext_x)).astype(jnp.float32) + 0.5
    coord_y = (lax.axis_index("gas") * ext_y + jnp.arange(ext_y)).astype(jnp.float32) + 0.5
    coord_z = jnp.arange(ext_z).astype(jnp.float32) + 0.5
    cell_place = jnp.stack(
        [
            jnp.broadcast_to(coord_x[:, None, None], grid_shape),
            jnp.broadcast_to(coord_y[None, :, None], grid_shape),
            jnp.broadcast_to(coord_z[None, None, :], grid_shape),
        ]
    ).reshape(3, -1)
    cell_mass = density.reshape(-1)
    order_rank = jnp.cumsum(is_mine.astype(jnp.int32)) - 1
    slot_iota = jnp.arange(MOST, dtype=jnp.int32)
    slot_pick = (is_mine[:, None] & (order_rank[:, None] == slot_iota[None, :])).astype(jnp.float32)
    selector = jnp.dot(owned, slot_pick, precision=highest)
    packed = jnp.dot(resident, selector, precision=highest)
    targets = lax.all_gather(packed, ("star", "gas"), axis=1, tiled=True)
    partial_terms, kick_sum = all_terms(targets, resident, cell_place, cell_mass)
    summed = lax.psum(partial_terms, ("star", "gas"))
    mine_terms = lax.dynamic_slice_in_dim(summed, my_rank * MOST, MOST, 1)
    own_terms = jnp.dot(mine_terms, selector.T, precision=highest)
    new_acc = own_terms[0:3]
    new_jerk = own_terms[3:6]
    vel_one = (
        star_vel
        + time_step * (old_acc + new_acc) / 2.0
        + time_step**2 * (old_jerk - new_jerk) / 12.0
    )
    pos_one = (
        star_pos
        + time_step * (star_vel + vel_one) / 2.0
        + time_step**2 * (old_acc - new_acc) / 12.0
    )
    updated = jnp.concatenate([pos_one, vel_one, new_acc, new_jerk], 0)
    base = jnp.concatenate([star_pos, star_vel, star_accel], 0)
    star_new = jnp.where(active_mask[None, :], updated, base)
    flow = flow_in + time_step * kick_sum.reshape(3, ext_x, ext_y, ext_z)

    def rate_of(values):
        padded = with_halo(
            jnp.concatenate([values, flow, density[None]], 0), (("star", 1), ("gas", 2)), 2
        )
        return field_rate(padded[0:3], padded[3:6], padded[6])

    first_section = field_in + field_step * rate_of(field_in)
    field_out = 0.5 * (field_in + first_section + field_step * rate_of(first_section))
    return (star_new, flow, field_out)


def solution(mesh):
    placed = (
        P(None, ("star", "gas")),
        P(None, ("star", "gas")),
        P(None, ("star", "gas")),
        P(("star", "gas")),
        P(),
        P("star", "gas", None),
        P(None, "star", "gas", None),
        P(None, "star", "gas", None),
    )
    return jax.shard_map(
        body,
        mesh=mesh,
        in_specs=placed,
        out_specs=(
            P(None, ("star", "gas")),
            P(None, "star", "gas", None),
            P(None, "star", "gas", None),
        ),
        check_vma=False,
    )
```

profile of v0, /device:TPU:1, one launch (start us, length us, event | category | flops | bytes accessed | tf_op | source)
XLA Modules:
  0.0 1057.4 jit_solution(8387592304197424626)
XLA Ops:
  7.3 0.7 add_select_fusion
  8.0 0.7 convert_bitcast_fusion
  9.3 1.4 fusion.14
  10.9 629.3 %all-gather = f32[256,24,7]{1,2,0:T(8,128)S(1)} all-gather(f32[1,24,7]{1,2,0:T(8,128)S(1)} %convolution_bitcast_fusion), channel_id=1, replica_groups=mesh['star'=64,'gas'=4] {'star','gas'}, dimensions={0}, use_global_device_ids=true | all-gather | bytes 172704 | tf_op jit(solution)/shard_map/all_gather | solution.py:143
  640.4 0.5 reshape.159
  641.8 144.5 %while.14 = (s32[]{:T(128)}, f32[3,2048]{1,0:T(4,128)S(1)}, f32[96,6,64]{2,1,0:T(8,128)S(1)}, f32[3,4,8,64]{3,2,1,0:T(8,128)}, f32[96,7,64]{2,0,1:T(8,128)S(1)},...) while((s32[]{:T(128)}, f32[3,2048]{1,0:T(4,128)S(1)}, ...), condition=%wide.wide.region_11.12_spmd.clone, body=%wide.wide.region_3.11_spmd.clone.sunk | while | flops 5353989 | bytes 4405187 | solution.py:102
  642.8 0.5 fusion.148
  644.3 0.5 fusion.148
  645.8 0.5 fusion.148
  647.3 0.5 fusion.148
  648.8 0.5 fusion.148
  650.3 0.5 fusion.148
  651.8 0.5 fusion.148
  653.3 0.5 fusion.148
  654.8 0.5 fusion.148
  656.3 0.5 fusion.148
  657.8 0.5 fusion.148
  659.3 0.5 fusion.148
  786.5 0.7 pad_maximum_fusion.9
  787.4 6.9 collective-permute-start.1
  794.3 0.8 reshape.156
  795.1 0.8 convert_reduce_fusion
  796.1 3.6 collective-permute-start.3
  799.7 1.9 collective-permute-done.2
  802.8 7.0 collective-permute-start.5
  809.8 231.5 %all-reduce.2.cloned.1.call-done = f32[6,6144]{1,0:T(8,128)} async-done(((f32[6,6144]{1,0:T(8,128)}), f32[6,6144]{1,0:T(8,128)}) %all-reduce.2.cloned.1.call-update) | async-done | bytes 147472 | tf_op jit(solution)/shard_map/psum | solution.py:145
  1041.2 0.9 fusion.97
  1042.2 0.9 collective-permute-start.6
  1043.1 2.7 collective-permute-start.7
  1045.9 0.6 maximum_select_fusion
  1046.5 2.1 collective-permute-done.6
  1049.9 0.6 fusion.58
  (1329 shorter events, 135.1 us)
Async XLA Ops:
  7.2 1034.1 %all-reduce.2.cloned.1.call-start = ((), (), s32[]{:S(2)}) async-start(), calls=%async_computation | async-start | bytes 393216 | tf_op jit(solution)/shard_map/psum | solution.py:145
  9.3 1.4 copy-start.5
  9.3 1.4 copy-start.7
  9.3 1.4 copy-start.8
  9.3 1.5 copy-start.6
  640.3 1.0 copy-start.2
  641.2 0.6 copy-start.4
  641.8 144.7 %copy-start.9 = (f32[3,4,8,64]{3,2,1,0:T(8,128)S(1)}, f32[3,4,8,64]{3,2,1,0:T(8,128)}, u32[]{:S(2)}) copy-start(f32[3,4,8,64]{3,2,1,0:T(8,128)} %param.16) | copy-start | bytes 73732
  641.8 144.7 %copy-start.1 = (f32[3,4,8,64]{3,2,1,0:T(8,128)S(1)}, f32[3,4,8,64]{3,2,1,0:T(8,128)}, u32[]{:S(2)}) copy-start(f32[3,4,8,64]{3,2,1,0:T(8,128)} %param.17) | copy-start | bytes 73732
  786.4 9.5 copy-start.3
  786.5 262.1 %copy-start = (f32[3,4,8,64]{3,2,1,0:T(8,128)}, f32[3,4,8,64]{3,2,1,0:T(8,128)S(1)}, u32[]{:S(2)}) copy-start(f32[3,4,8,64]{3,2,1,0:T(8,128)S(1)} %add.174) | copy-start | bytes 73732
  787.3 8.6 collective-permute-start
  787.4 8.5 collective-permute-start.1
  796.0 5.5 collective-permute-start.2
  796.1 5.4 collective-permute-start.3
  802.7 239.5 %collective-permute-start.4 = (f32[7,2,8,64]{3,2,1,0:T(8,128)S(1)}, f32[7,2,8,64]{3,2,1,0:T(8,128)S(1)}, u32[]{:S(2)}, u32[]{:S(2)}) collective-permute-start(f32[7,2,8,64]{3,2,1,0:T(8,128)S(1)} %get-tuple-element.178), channel_id=1, source_target_pairs={{0,4},{4,8},{8,12},{12,16},{16,20},{20,24},{24,28},{28,32},{32,36}... | collective-permute-start | bytes 86024 | tf_op jit(solution)/shard_map/ppermute | solution.py:21
  802.8 239.4 %collective-permute-start.5 = (f32[7,2,8,64]{3,2,1,0:T(8,128)S(1)}, f32[7,2,8,64]{3,2,1,0:T(8,128)S(1)}, u32[]{:S(2)}, u32[]{:S(2)}) collective-permute-start(f32[7,2,8,64]{3,2,1,0:T(8,128)S(1)} %get-tuple-element.179), channel_id=1, source_target_pairs={{4,0},{8,4},{12,8},{16,12},{20,16},{24,20},{28,24},{32,28},{36,32}... | collective-permute-start | bytes 86024 | tf_op jit(solution)/shard_map/ppermute | solution.py:24
  1042.2 6.4 collective-permute-start.6
  1043.1 5.5 collective-permute-start.7
Sparse Core Ops, SparseCore 0:
  795.3 245.9 all-reduce.1
where the time goes:
time: 1060 us
  blocking collectives  629 us (59%)
  waiting for transfers between devices  235 us (22%)
  other arithmetic  139 us (13%)
  starting transfers between devices  21.4 us (2%)
  between operations  14.4 us (1%)
    all_gather x1, blocking collectives, body(): targets = lax.all_gather(packed, ('star', 'gas'), axis=1, tiled=True)  629 us
    psum x1, waiting for transfers between devices, body(): summed = lax.psum(partial_terms, ('star', 'gas'))  231 us
    reduce_sum x96, other arithmetic, pair_terms(): gas_acc = jnp.sum((inv_cube * cell_mass[None, :])[None] * cell_gap, 2)  48.2 us
    reduce_sum x96, other arithmetic, pair_terms(): star_acc = jnp.sum(weight[None] * star_gap, 2)  27.3 us
  transfers between devices with their start and end apart: 9, of which 3 were waited for; matrix products, arithmetic and copies ran while one was open for 0% of the time, Pallas kernels for 0%

commit v1 on v0

--- a/solution.py
+++ b/solution.py
@@ -3,6 +3,7 @@
 import jax.numpy as jnp
 from jax import lax
 from jax.sharding import PartitionSpec as P
+from jax.lax import all_to_all, axis_size
 
 MOST = 24
 gravity = 0.02
@@ -10,6 +11,13 @@
 time_step = 1.5
 field_step = 0.1
 highest = lax.Precision.HIGHEST
+
+
+def list_row_by_axis(message):
+    u1 = jnp.concatenate(
+        all_to_all(jnp.stack([message] * axis_size(("star", "gas")), 0), ("star", "gas"), 0, 0), 1
+    )
+    return u1
 
 
 def with_halo(block, sides, width):
@@ -140,7 +148,7 @@
     slot_pick = (is_mine[:, None] & (order_rank[:, None] == slot_iota[None, :])).astype(jnp.float32)
     selector = jnp.dot(owned, slot_pick, precision=highest)
     packed = jnp.dot(resident, selector, precision=highest)
-    targets = lax.all_gather(packed, ("star", "gas"), axis=1, tiled=True)
+    targets = list_row_by_axis(packed)
     partial_terms, kick_sum = all_terms(targets, resident, cell_place, cell_mass)
     summed = lax.psum(partial_terms, ("star", "gas"))
     mine_terms = lax.dynamic_slice_in_dim(summed, my_rank * MOST, MOST, 1)

time: 1060 us -> 468 us (0.44)
  blocking collectives: 629 us -> 0 us
  waiting for transfers between devices: 235 us -> 263 us
    all_gather x1 -> x0, blocking collectives: 629 us -> none  [body(): targets = lax.all_gather(packed, ('star', 'gas'), axis=1, tiled=True)]
    all_to_all x0 -> x1, starting transfers between devices: none -> 15.6 us  [list_row_by_axis(): all_to_all(jnp.stack([message] * axis_size(('star', 'gas')), 0), ('star',...]
    all_to_all x0 -> x1, waiting for transfers between devices: none -> 14.8 us  [list_row_by_axis(): all_to_all(jnp.stack([message] * axis_size(('star', 'gas')), 0), ('star',...]
    ppermute x4, starting transfers between devices: 20.2 us -> 8.01 us  [with_halo(): lax.ppermute(lax.slice_in_dim(block, 0, width, axis=dim), axis, backward)]
    psum x1, waiting for transfers between devices: 231 us -> 242 us  [body(): summed = lax.psum(partial_terms, ('star', 'gas'))]
  transfers between devices with their start and end apart: 9 -> 10, of which waited for: 3 -> 7; matrix products, arithmetic and copies ran while one was open for 0% -> 1% of each run, Pallas kernels for 0% -> 0%
where the time goes in v1:
time: 468 us
  waiting for transfers between devices  263 us (56%)
  other arithmetic  141 us (30%)
  starting transfers between devices  29.3 us (6%)
  between operations  14.4 us (3%)
  local copies, waits for them, and re-layouts  8.64 us (2%)
  loops' own time  8.23 us (2%)
    psum x1, waiting for transfers between devices, body(): summed = lax.psum(partial_terms, ('star', 'gas'))  242 us
    reduce_sum x96, other arithmetic, pair_terms(): gas_acc = jnp.sum((inv_cube * cell_mass[None, :])[None] * cell_gap, 2)  48.2 us
    reduce_sum x96, other arithmetic, pair_terms(): star_acc = jnp.sum(weight[None] * star_gap, 2)  27.3 us
    reduce_sum x96, other arithmetic, pair_terms(): inv_g = lax.rsqrt(jnp.sum(cell_gap * cell_gap, 0) + soften)  21.1 us
    all_to_all x1, starting transfers between devices, list_row_by_axis(): all_to_all(jnp.stack([message] * axis_size(('star', 'gas')), 0), ('star',...  15.6 us
    all_to_all x1, waiting for transfers between devices, list_row_by_axis(): all_to_all(jnp.stack([message] * axis_size(('star', 'gas')), 0), ('star',...  14.8 us
    mul x96, other arithmetic, pair_terms(): cell_kick = -jnp.sum((inv_cube * target[6][:, None])[None] * cell_gap, 1)  14.6 us
    reduce_sum x96, other arithmetic, pair_terms(): inv_r = lax.rsqrt(jnp.sum(star_gap * star_gap, 0) + soften)  13.4 us
  transfers between devices with their start and end apart: 10, of which 7 were waited for; matrix products, arithmetic and copies ran while one was open for 1% of the time, Pallas kernels for 0%

profile of v1, /device:TPU:1, one launch (start us, length us, event | category | flops | bytes accessed | tf_op | source)
XLA Modules:
  0.0 467.8 jit_solution(18409032793383858442)
XLA Ops:
  7.2 0.7 add_select_fusion
  7.9 0.7 convert_bitcast_fusion
  9.2 1.4 fusion.14
  10.9 1.4 reshape.161
  12.3 15.6 %all-to-all-start = ((f32[256,1,168]{2,1,0:T(1,128)}), f32[256,1,168]{2,1,0:T(1,128)S(1)}, u32[]{:S(2)}, u32[]{:S(2)}) async-start(f32[256,1,168]{2,1,0:T(1,128)} %reshape.161), calls=%async_computation | async-start | bytes 524288 | tf_op jit(solution)/shard_map/all_to_all | solution.py:18
  28.4 14.8 %all-to-all-done = f32[256,1,168]{2,1,0:T(1,128)S(1)} async-done(((f32[256,1,168]{2,1,0:T(1,128)}), f32[256,1,168]{2,1,0:T(1,128)S(1)}, u32[]{:S(2)}, u32[]{:S(2)}) %all-to-all-start) | async-done | bytes 172064 | tf_op jit(solution)/shard_map/all_to_all | solution.py:18
  43.2 0.5 broadcast.239
  43.7 1.3 reduce.2
  46.1 144.6 %while.14 = (s32[]{:T(128)}, f32[3,2048]{1,0:T(4,128)S(1)}, f32[96,6,64]{2,1,0:T(8,128)S(1)}, f32[3,4,8,64]{3,2,1,0:T(8,128)}, f32[96,7,64]{2,0,1:T(8,128)S(1)},...) while((s32[]{:T(128)}, f32[3,2048]{1,0:T(4,128)S(1)}, ...), condition=%wide.wide.region_11.12_spmd.clone, body=%wide.wide.region_3.11_spmd.clone.sunk | while | flops 5353989 | bytes 4405187 | solution.py:110
  47.0 0.5 fusion.149
  48.5 0.5 fusion.149
  50.0 0.5 fusion.149
  51.5 0.5 fusion.149
  53.0 0.5 fusion.149
  190.8 0.7 pad_maximum_fusion.9
  192.1 0.8 convert_reduce_fusion
  193.3 2.3 collective-permute-done.1
  195.6 0.7 fusion.31
  196.4 1.8 collective-permute-start.2
  198.3 1.8 collective-permute-start.3
  200.1 0.8 reshape.158
  200.9 0.7 collective-permute-done.2
  201.7 0.6 collective-permute-done.3
  203.5 2.4 collective-permute-start.4
  205.8 3.3 collective-permute-start.5
  209.2 242.5 %all-reduce.2.cloned.1.call-done = f32[6,6144]{1,0:T(8,128)} async-done(((f32[6,6144]{1,0:T(8,128)}), f32[6,6144]{1,0:T(8,128)}) %all-reduce.2.cloned.1.call-update) | async-done | bytes 147472 | tf_op jit(solution)/shard_map/psum | solution.py:153
  451.6 0.9 fusion.98
  452.7 0.9 collective-permute-start.6
  453.6 2.7 collective-permute-start.7
  456.3 0.6 maximum_select_fusion
  457.0 2.1 collective-permute-done.6
  460.3 0.6 fusion.58
  (1334 shorter events, 139.6 us)
Async XLA Ops:
  9.2 1.4 copy-start.5
  9.2 1.4 copy-start.7
  9.2 1.4 copy-start.8
  9.2 1.5 copy-start.6
  10.9 17.4 %copy-start.2 = (f32[4,8,64]{2,1,0:T(8,128)S(1)}, f32[4,8,64]{2,1,0:T(8,128)}, u32[]{:S(2)}) copy-start(f32[4,8,64]{2,1,0:T(8,128)} %param.15) | copy-start | bytes 24580
  12.3 30.9 %all-to-all-start = ((f32[256,1,168]{2,1,0:T(1,128)}), f32[256,1,168]{2,1,0:T(1,128)S(1)}, u32[]{:S(2)}, u32[]{:S(2)}) async-start(f32[256,1,168]{2,1,0:T(1,128)} %reshape.161), calls=%async_computation | async-start | bytes 524288 | tf_op jit(solution)/shard_map/all_to_all | solution.py:18
  28.0 423.7 %all-reduce.2.cloned.1.call-start = ((), (), s32[]{:S(2)}) async-start(), calls=%async_computation.1 | async-start | bytes 393216 | tf_op jit(solution)/shard_map/psum | solution.py:153
  28.2 17.3 %copy-start.4 = (f32[3,4,8,64]{3,2,1,0:T(8,128)}, f32[3,4,8,64]{3,2,1,0:T(8,128)S(1)}, u32[]{:S(2)}) copy-start(f32[3,4,8,64]{3,2,1,0:T(8,128)S(1)} %pad_maximum_fusion.20) | copy-start | bytes 73732
  46.0 144.7 %copy-start.9 = (f32[3,4,8,64]{3,2,1,0:T(8,128)S(1)}, f32[3,4,8,64]{3,2,1,0:T(8,128)}, u32[]{:S(2)}) copy-start(f32[3,4,8,64]{3,2,1,0:T(8,128)} %param.16) | copy-start | bytes 73732
  46.1 144.7 %copy-start.1 = (f32[3,4,8,64]{3,2,1,0:T(8,128)S(1)}, f32[3,4,8,64]{3,2,1,0:T(8,128)}, u32[]{:S(2)}) copy-start(f32[3,4,8,64]{3,2,1,0:T(8,128)} %param.17) | copy-start | bytes 73732
  190.8 268.3 %copy-start = (f32[3,4,8,64]{3,2,1,0:T(8,128)}, f32[3,4,8,64]{3,2,1,0:T(8,128)S(1)}, u32[]{:S(2)}) copy-start(f32[3,4,8,64]{3,2,1,0:T(8,128)S(1)} %add.174) | copy-start | bytes 73732
  191.5 1.7 collective-permute-start
  192.0 10.3 %copy-start.3 = (f32[4,8,64]{2,1,0:T(8,128)S(1)}, f32[4,8,64]{2,1,0:T(8,128)}, u32[]{:S(2)}) copy-start(f32[4,8,64]{2,1,0:T(8,128)} %get-tuple-element.415) | copy-start | bytes 24580
  192.0 3.6 collective-permute-start.1
  196.4 5.3 %collective-permute-start.2 = (f32[7,8,2,64]{3,2,1,0:T(2,128)S(1)}, f32[7,8,2,64]{3,2,1,0:T(2,128)S(1)}, u32[]{:S(2)}, u32[]{:S(2)}) collective-permute-start(f32[7,8,2,64]{3,2,1,0:T(2,128)S(1)} %get-tuple-element.176), channel_id=1, source_target_pairs={{0,1},{1,2},{2,3},{3,0},{4,5},{5,6},{6,7},{7,4},{8,9},{9,10},{10,1... | collective-permute-start | bytes 86024 | tf_op jit(solution)/shard_map/ppermute | solution.py:29
  198.3 4.1 collective-permute-start.3
  203.5 249.1 %collective-permute-start.4 = (f32[7,2,8,64]{3,2,1,0:T(8,128)S(1)}, f32[7,2,8,64]{3,2,1,0:T(8,128)S(1)}, u32[]{:S(2)}, u32[]{:S(2)}) collective-permute-start(f32[7,2,8,64]{3,2,1,0:T(8,128)S(1)} %get-tuple-element.178), channel_id=1, source_target_pairs={{0,4},{4,8},{8,12},{12,16},{16,20},{20,24},{24,28},{28,32},{32,36}... | collective-permute-start | bytes 86024 | tf_op jit(solution)/shard_map/ppermute | solution.py:29
  205.8 246.8 %collective-permute-start.5 = (f32[7,2,8,64]{3,2,1,0:T(8,128)S(1)}, f32[7,2,8,64]{3,2,1,0:T(8,128)S(1)}, u32[]{:S(2)}, u32[]{:S(2)}) collective-permute-start(f32[7,2,8,64]{3,2,1,0:T(8,128)S(1)} %get-tuple-element.179), channel_id=1, source_target_pairs={{4,0},{8,4},{12,8},{16,12},{20,16},{24,20},{28,24},{32,28},{36,32}... | collective-permute-start | bytes 86024 | tf_op jit(solution)/shard_map/ppermute | solution.py:32
  452.7 6.4 %collective-permute-start.6 = (f32[7,8,2,64]{3,2,1,0:T(2,128)S(1)}, f32[7,8,2,64]{3,2,1,0:T(2,128)S(1)}, u32[]{:S(2)}, u32[]{:S(2)}) collective-permute-start(f32[7,8,2,64]{3,2,1,0:T(2,128)S(1)} %get-tuple-element.174), channel_id=1, source_target_pairs={{0,1},{1,2},{2,3},{3,0},{4,5},{5,6},{6,7},{7,4},{8,9},{9,10},{10,1... | collective-permute-start | bytes 86024 | tf_op jit(solution)/shard_map/ppermute | solution.py:29
  453.6 5.5 %collective-permute-start.7 = (f32[7,8,2,64]{3,2,1,0:T(2,128)S(1)}, f32[7,8,2,64]{3,2,1,0:T(2,128)S(1)}, u32[]{:S(2)}, u32[]{:S(2)}) collective-permute-start(f32[7,8,2,64]{3,2,1,0:T(2,128)S(1)} %get-tuple-element.175), channel_id=1, source_target_pairs={{1,0},{2,1},{3,2},{0,3},{5,4},{6,5},{7,6},{4,7},{9,8},{10,9},{11,1... | collective-permute-start | bytes 86024 | tf_op jit(solution)/shard_map/ppermute | solution.py:32
Sparse Core Ops, SparseCore 0:
  201.1 250.5 all-reduce.1
